TPU v7x, 128 devices: a whole 4x4x4 slice. The times are simulated.
128 devices in a mesh: section: 2 (over x_lo), expert: 16 (over z, x_hi, core), dp: 4 (over y).
Axes of the slice: x: 4 (x_hi: 2, x_lo: 2; x = x_hi * 2 + x_lo), y: 4, z: 4, core: 2. Of those that a mesh axis runs over, the one named last changes fastest.
Arguments:
- fresh_tokens: bfloat16 [2, 4096, 4096], P(None, ('expert', 'dp')), may hold values from -60 to 60
- in_flight: bfloat16 [4096, 4096], P(('expert', 'dp')), may hold values from -60 to 60
- norm_weight: float32 [2, 4096], P('section'), may hold values from 0.1 to 1.9
- gate_up: bfloat16 [2, 16, 2, 4096, 768], P('section', 'expert', None, 'dp'), may hold values from -0.09375 to 0.09375
- down_proj: bfloat16 [2, 16, 768, 4096], P('section', 'expert', 'dp'), may hold values from -0.21875 to 0.21875
- first_moment: bfloat16 [2, 16, 768, 4096], P('section', 'expert', 'dp'), may hold values from -6 to 6
- second_moment: bfloat16 [2, 16, 768, 4096], P('section', 'expert', 'dp'), may hold values from 0.099609375 to 4
- route_ids: int32 [2, 2, 4096, 8], P('section', None, ('expert', 'dp')), may hold values from 0 to 15, all different within a row; in each aligned block of 64 rows (0 to 63, 64 to 127, ..., all dimensions but the last counted through in order) at most 36 rows name the same one
- route_probs: float32 [2, 2, 4096, 8], P('section', None, ('expert', 'dp')), may hold values from 0.05 to 1
- trade_flags: int32 [8, 1], replicated, may hold values from 0 to 1, as said below
Outputs:
- layer_out: bfloat16 [2, 2, 4096, 4096], P('section', None, ('expert', 'dp'))
- gate_up_moved: bfloat16 [2, 16, 2, 4096, 768], P('section', 'expert', None, 'dp')
- down_moved: bfloat16 [2, 16, 768, 4096], P('section', 'expert', 'dp')
- first_moved: bfloat16 [2, 16, 768, 4096], P('section', 'expert', 'dp')
- second_moved: bfloat16 [2, 16, 768, 4096], P('section', 'expert', 'dp')
Inputs may be any that keep to these rules, and one draw needn't show every extreme that they name: `route_ids`: in each aligned block of 64 rows (one device's tokens of one section and tick) the 8 experts of a token differ and no expert is chosen by more than 36 rows. `trade_flags`: at least one entry is 1 and at least one is 0.
All inputs are finite; a program needn't handle non-finite values.
Results may differ from a plain program's by a relative error of at most 0.0035.
Values may be sent and summed in bfloat16 or wider, within the bound.
A program may use at most 128 MiB of HBM per device.

v0:
```python
import jax
import jax.numpy as jnp
from jax import lax
from jax.sharding import PartitionSpec as P

EXPERTS = 16


def partner(value, axis, bit):
    return lax.ppermute(value, axis, [(i, i ^ 1 << bit) for i in range(lax.axis_size(axis))])


def shifted(block, axis, distance):
    devices = range(lax.axis_size(axis))
    route = [(i - distance, i) for i in devices if i - distance in devices]
    return lax.ppermute(block, axis, route)


def rms_normed(inputs, norm_gain):
    values = inputs.astype(jnp.float32)
    inverse_rms = lax.rsqrt(jnp.mean(values * values, axis=-1, keepdims=True) + 1e-06)
    return (values * inverse_rms * norm_gain).astype(jnp.bfloat16)


def per_device(
    fresh_tokens,
    in_flight,
    norm_weight,
    gate_up,
    down_proj,
    first_moment,
    second_moment,
    route_ids,
    route_probs,
    trade_flags,
):
    groups = lax.axis_size("expert")
    half_span = groups // 2
    top_bit = groups.bit_length() - 2
    own_rank = lax.axis_index("expert")
    section_index = lax.axis_index("section")
    full_gate_up = lax.all_gather(gate_up, "dp", axis=3, tiled=True)
    full_down = lax.all_gather(down_proj, "dp", axis=2, tiled=True)
    gate_weights = full_gate_up[0, 0, 0]
    up_weights = full_gate_up[0, 0, 1]
    down_weights = full_down[0, 0]
    expert_ids = jnp.arange(EXPERTS, dtype=jnp.int32)
    probs = route_probs[0]
    mix = probs / jnp.sum(probs, axis=-1, keepdims=True)
    chosen = route_ids[0][:, :, :, None] == expert_ids
    dense_mix = jnp.sum(jnp.where(chosen, mix[:, :, :, None], 0.0), axis=2)
    all_mix = lax.all_gather(dense_mix, "expert", axis=1, tiled=True)
    own_mix = jnp.sum(jnp.where(expert_ids == own_rank, all_mix, 0.0), axis=-1)
    traded = partner((gate_up, down_proj, first_moment, second_moment), "expert", top_bit)

    def layer(inputs, scale, held=None):
        normed = rms_normed(inputs, norm_weight[0])
        arrived = lax.all_gather(normed, "expert", axis=0, tiled=True)
        gate_part = jnp.dot(arrived, gate_weights, preferred_element_type=jnp.float32)
        up_part = jnp.dot(arrived, up_weights, preferred_element_type=jnp.float32)
        active = (jax.nn.silu(gate_part) * up_part).astype(jnp.bfloat16)
        result = jnp.dot(active, down_weights, preferred_element_type=jnp.float32)
        result = (result * scale[:, None]).astype(jnp.bfloat16)
        if held is not None:
            result, held = lax.optimization_barrier((result, held))
        combined = lax.psum_scatter(result, "expert", scatter_dimension=0, tiled=True)
        return (
            (inputs.astype(jnp.float32) + combined.astype(jnp.float32)).astype(jnp.bfloat16),
            held,
        )

    first_input = jnp.where(section_index == 0, fresh_tokens[0], in_flight)
    tick_zero, traded = layer(first_input, own_mix[0], traded)
    arrived = shifted(tick_zero, "section", 1)
    second_input = jnp.where(section_index == 0, fresh_tokens[1], arrived)
    tick_one, _ = layer(second_input, own_mix[1])
    layer_out = jnp.stack([tick_zero, tick_one])[None]
    own_flags = trade_flags[own_rank % half_span] == 1
    mask_five = own_flags[None, :, None, None, None]
    mask_four = own_flags[None, :, None, None]
    gate_up_moved = jnp.where(mask_five, traded[0], gate_up)
    down_moved = jnp.where(mask_four, traded[1], down_proj)
    first_moved = jnp.where(mask_four, traded[2], first_moment)
    second_moved = jnp.where(mask_four, traded[3], second_moment)
    return (layer_out, gate_up_moved, down_moved, first_moved, second_moved)


def solution(mesh):
    return jax.shard_map(
        per_device,
        mesh=mesh,
        in_specs=(
            P(None, ("expert", "dp"), None),
            P(("expert", "dp"), None),
            P("section", None),
            P("section", "expert", None, "dp", None),
            P("section", "expert", "dp", None),
            P("section", "expert", "dp", None),
            P("section", "expert", "dp", None),
            P("section", None, ("expert", "dp"), None),
            P("section", None, ("expert", "dp"), None),
            P(),
        ),
        out_specs=(
            P("section", None, ("expert", "dp"), None),
            P("section", "expert", None, "dp", None),
            P("section", "expert", "dp", None),
            P("section", "expert", "dp", None),
            P("section", "expert", "dp", None),
        ),
        check_vma=False,
    )
```

profile of v0, /device:TPU:0, one launch (start us, length us, event | category | flops | bytes accessed | tf_op | source)
XLA Modules:
  0.0 780.1 jit_solution(14578231850789856475)
XLA Ops:
  7.2 1.3 fusion.6
  9.4 1.8 fusion.8
  12.8 4.0 collective-permute-start.1
  16.9 3.4 collective-permute-start.2
  20.6 35.1 %all_gather.18 = f32[2,1024,16]{2,0,1:T(2,128)S(1)} all-gather(f32[2,64,16]{2,0,1:T(2,128)S(1)} %copy.17), channel_id=1, replica_groups=mesh['section'=2,'expert'=16,'dp'=4] {'expert'}, dimensions={1}, use_global_device_ids=true | all-gather | bytes 139264 | tf_op jit(solution)/shard_map/all_gather | solution.py:52
  55.7 1.2 select_reduce_fusion
  56.9 1.1 fusion.15
  58.0 1.2 copy.20
  59.2 187.8 %all-gather.5.cloned.1.call-done = bf16[1024,4096]{1,0:T(8,128)(2,1)} async-done(((bf16[64,4096]{1,0:T(8,128)(2,1)}), bf16[1024,4096]{1,0:T(8,128)(2,1)}) %all-gather.5.cloned.1.call-update) | async-done | bytes 8388624 | tf_op jit(solution)/shard_map/all_gather | solution.py:58
  247.0 118.0 %all-gather.7.cloned.1.call-done = bf16[1,1,2,4096,768]{4,3,2,1,0:T(8,128)(2,1)} async-done(((bf16[1,1,2,1024,768]{4,3,2,1,0:T(8,128)(2,1)}), bf16[1,1,2,4096,768]{4,3,2,1,0:T(8,128)(2,1)}) %all-gather.7.cloned.1.call-update) | async-done | bytes 12582928 | tf_op jit(solution)/shard_map/all_gather | solution.py:42
  365.0 11.0 %fusion.5 = f32[1024,768]{1,0:T(8,128)S(1)} fusion(bf16[1024,4096]{1,0:T(8,128)(2,1)} %all-gather.5.cloned.1.call-done, bf16[1,1,2,4096,768]{4,3,2,1,0:T(8,128)(2,1)} %all-gather.7.cloned.1.call-done), kind=kOutput, calls=%fused_computation.9 | convolution fusion | flops 6442450944 | bytes 17825792 | tf_op jit(solution)/shard_map/dot_general | solution.py:60
  376.2 8.1 %multiply_convert_fusion.3 = bf16[1024,768]{1,0:T(8,128)(2,1)} fusion(f32[1024,768]{1,0:T(8,128)S(1)} %fusion.5, bf16[1024,4096]{1,0:T(8,128)(2,1)S(1)} %copy-done.13, bf16[1,1,2,4096,768]{4,3,2,1,0:T(8,128)(2,1)S(1)} %copy-done.12), kind=kOutput, calls=%fused_computation.11 | convolution fusion | flops 6447169536 | bytes 19398656 | tf_op jit(solution)/shard_map/dot_general | solution.py:59
  384.2 49.1 %all-gather.9.cloned.1.call-done = bf16[1,1,768,4096]{3,2,1,0:T(8,128)(2,1)} async-done(((bf16[1,1,192,4096]{3,2,1,0:T(8,128)(2,1)}), bf16[1,1,768,4096]{3,2,1,0:T(8,128)(2,1)}) %all-gather.9.cloned.1.call-update) | async-done | bytes 6291472 | tf_op jit(solution)/shard_map/all_gather | solution.py:43
  433.4 11.2 %multiply_convert_fusion.1 = bf16[1024,4096]{1,0:T(8,128)(2,1)} fusion(f32[1024]{0:T(1024)S(1)} %bitcast.45, bf16[1024,768]{1,0:T(8,128)(2,1)} %multiply_convert_fusion.3, bf16[1,1,768,4096]{3,2,1,0:T(8,128)(2,1)} %all-gather.9.cloned.1.call-done), kind=kOutput, calls=%fused_computation.1 | convolution fusion | flops 6450839552 | bytes 16257024 | tf_op jit(solution)/shard_map/dot_general | solution.py:62
  444.7 103.2 %reduce-scatter.3.cloned.1.call-done = bf16[64,4096]{1,0:T(8,128)(2,1)} async-done(((bf16[1024,4096]{1,0:T(8,128)(2,1)}), bf16[64,4096]{1,0:T(8,128)(2,1)}) %reduce-scatter.3.cloned.1.call-update) | async-done | bytes 524304 | tf_op jit(solution)/shard_map/reduce_scatter | solution.py:66
  547.9 1.3 fusion.9
  549.3 2.5 collective-permute-start.4
  551.8 10.1 %collective-permute-done.4 = bf16[64,4096]{1,0:T(8,128)(2,1)S(1)} collective-permute-done((bf16[64,4096]{1,0:T(8,128)(2,1)S(1)}, bf16[64,4096]{1,0:T(8,128)(2,1)S(1)}, u32[]{:S(2)}, u32[]{:S(2)}) %collective-permute-start.4) | collective-permute-done | bytes 524320 | tf_op jit(solution)/shard_map/ppermute | solution.py:16
  561.9 1.3 fusion.10
  563.2 0.8 copy-done.3
  564.0 1.0 fusion.12
  565.3 1.2 copy.21
  566.5 71.6 %all-gather.11.cloned.1.call-done = bf16[1024,4096]{1,0:T(8,128)(2,1)} async-done(((bf16[64,4096]{1,0:T(8,128)(2,1)}), bf16[1024,4096]{1,0:T(8,128)(2,1)}) %all-gather.11.cloned.1.call-update) | async-done | bytes 8388624 | tf_op jit(solution)/shard_map/all_gather | solution.py:58
  638.1 11.0 %fusion.4 = f32[1024,768]{1,0:T(8,128)S(1)} fusion(bf16[1024,4096]{1,0:T(8,128)(2,1)} %all-gather.11.cloned.1.call-done, bf16[1,1,2,4096,768]{4,3,2,1,0:T(8,128)(2,1)} %all-gather.7.cloned.1.call-done), kind=kOutput, calls=%fused_computation.8 | convolution fusion | flops 6442450944 | bytes 17825792 | tf_op jit(solution)/shard_map/dot_general | solution.py:60
  649.1 9.8 %multiply_convert_fusion.2 = bf16[1024,768]{1,0:T(8,128)(2,1)S(1)} fusion(f32[1024,768]{1,0:T(8,128)S(1)} %fusion.4, bf16[1024,4096]{1,0:T(8,128)(2,1)S(1)} %copy-done.14, bf16[1,1,2,4096,768]{4,3,2,1,0:T(8,128)(2,1)} %all-gather.7.cloned.1.call-done), kind=kOutput, calls=%fused_computation.10 | convolution fusion | flops 6447169536 | bytes 19398656 | tf_op jit(solution)/shard_map/dot_general | solution.py:59
  658.9 11.7 %multiply_convert_fusion = bf16[1024,4096]{1,0:T(8,128)(2,1)} fusion(f32[1024]{0:T(1024)S(1)} %bitcast.46, bf16[1024,768]{1,0:T(8,128)(2,1)S(1)} %multiply_convert_fusion.2, bf16[1,1,768,4096]{3,2,1,0:T(8,128)(2,1)} %all-gather.9.cloned.1.call-done), kind=kOutput, calls=%fused_computation | convolution fusion | flops 6450839552 | bytes 16257024 | tf_op jit(solution)/shard_map/dot_general | solution.py:62
  671.9 4.6 broadcast_select_fusion
  676.6 4.0 broadcast_select_fusion.3
  680.5 4.9 broadcast_select_fusion.1
  685.4 85.6 %reduce-scatter.5.cloned.1.call-done = bf16[64,4096]{1,0:T(8,128)(2,1)} async-done(((bf16[1024,4096]{1,0:T(8,128)(2,1)}), bf16[64,4096]{1,0:T(8,128)(2,1)}) %reduce-scatter.5.cloned.1.call-update) | async-done | bytes 524304 | tf_op jit(solution)/shard_map/reduce_scatter | solution.py:66
  771.0 1.2 fusion.14
  772.2 1.1 maximum_bitcast_fusion
  (57 shorter events, 4.4 us)
Async XLA Ops:
  7.2 239.8 %all-gather.5.cloned.1.call-start = ((), (), s32[]{:S(2)}) async-start(), calls=%async_computation.2 | async-start | bytes 8912896 | tf_op jit(solution)/shard_map/all_gather | solution.py:58
  8.6 0.8 copy-start.2
  9.4 7.5 copy-start
  9.4 11.1 %copy-start.10 = (f32[1,2,64,8]{2,3,1,0:T(8,128)S(1)}, f32[1,2,64,8]{2,3,1,0:T(8,128)}, u32[]{:S(2)}) copy-start(f32[1,2,64,8]{2,3,1,0:T(8,128)} %param.18) | copy-start | bytes 12292
  9.4 11.1 %copy-start.11 = (s32[1,2,64,8]{2,3,1,0:T(8,128)S(1)}, s32[1,2,64,8]{2,3,1,0:T(8,128)}, u32[]{:S(2)}) copy-start(s32[1,2,64,8]{2,3,1,0:T(8,128)} %param.17) | copy-start | bytes 12292
  11.2 353.7 %all-gather.7.cloned.1.call-start = ((), (), s32[]{:S(2)}) async-start(), calls=%async_computation.3 | async-start | bytes 15728640 | tf_op jit(solution)/shard_map/all_gather | solution.py:42
  12.0 421.4 %all-gather.9.cloned.1.call-start = ((), (), s32[]{:S(2)}) async-start(), calls=%async_computation.4 | async-start | bytes 7864320 | tf_op jit(solution)/shard_map/all_gather | solution.py:43
  12.7 535.2 %reduce-scatter.3.cloned.1.call-start = ((), (), s32[]{:S(2)}) async-start(), calls=%async_computation.5 | async-start | bytes 8912896 | tf_op jit(solution)/shard_map/reduce_scatter | solution.py:66
  12.8 431.9 %collective-permute-start.1 = (bf16[1,1,192,4096]{3,2,1,0:T(8,128)(2,1)}, bf16[1,1,192,4096]{3,2,1,0:T(8,128)(2,1)}, u32[]{:S(2)}, u32[]{:S(2)}) collective-permute-start(bf16[1,1,192,4096]{3,2,1,0:T(8,128)(2,1)} %param.14), channel_id=1, source_target_pairs={{0,32},{4,36},{8,40},{12,44},{16,48},{20,52},{24,56},{28,60},{32,0... | collective-permute-start | bytes 4718600 | tf_op jit(solution)/shard_map/ppermute | solution.py:10
  16.8 427.8 %collective-permute-start = (bf16[1,1,2,1024,768]{4,3,2,1,0:T(8,128)(2,1)S(1)}, bf16[1,1,2,1024,768]{4,3,2,1,0:T(8,128)(2,1)}, u32[]{:S(2)}, u32[]{:S(2)}) collective-permute-start(bf16[1,1,2,1024,768]{4,3,2,1,0:T(8,128)(2,1)S(1)} %copy-done), channel_id=1, source_target_pairs={{0,32},{4,36},{8,40},{12,44},{16,48},{20,52},{24,56},{28,60},{32,0... | collective-permute-start | bytes 9437192 | tf_op jit(solution)/shard_map/ppermute | solution.py:10
  16.9 427.7 %collective-permute-start.2 = (bf16[1,1,192,4096]{3,2,1,0:T(8,128)(2,1)}, bf16[1,1,192,4096]{3,2,1,0:T(8,128)(2,1)}, u32[]{:S(2)}, u32[]{:S(2)}) collective-permute-start(bf16[1,1,192,4096]{3,2,1,0:T(8,128)(2,1)} %param.15), channel_id=1, source_target_pairs={{0,32},{4,36},{8,40},{12,44},{16,48},{20,52},{24,56},{28,60},{32,0... | collective-permute-start | bytes 4718600 | tf_op jit(solution)/shard_map/ppermute | solution.py:10
  20.3 424.3 %collective-permute-start.3 = (bf16[1,1,192,4096]{3,2,1,0:T(8,128)(2,1)}, bf16[1,1,192,4096]{3,2,1,0:T(8,128)(2,1)}, u32[]{:S(2)}, u32[]{:S(2)}) collective-permute-start(bf16[1,1,192,4096]{3,2,1,0:T(8,128)(2,1)} %param.16), channel_id=1, source_target_pairs={{0,32},{4,36},{8,40},{12,44},{16,48},{20,52},{24,56},{28,60},{32,0... | collective-permute-start | bytes 4718600 | tf_op jit(solution)/shard_map/ppermute | solution.py:10
  365.0 11.0 %copy-start.12 = (bf16[1,1,2,4096,768]{4,3,2,1,0:T(8,128)(2,1)S(1)}, bf16[1,1,2,4096,768]{4,3,2,1,0:T(8,128)(2,1)}, u32[]{:S(2)}) copy-start(bf16[1,1,2,4096,768]{4,3,2,1,0:T(8,128)(2,1)} %all-gather.7.cloned.1.call-done) | copy-start | bytes 37748740
  365.0 11.2 %copy-start.13 = (bf16[1024,4096]{1,0:T(8,128)(2,1)S(1)}, bf16[1024,4096]{1,0:T(8,128)(2,1)}, u32[]{:S(2)}) copy-start(bf16[1024,4096]{1,0:T(8,128)(2,1)} %all-gather.5.cloned.1.call-done) | copy-start | bytes 25165828
  444.7 119.3 %copy-start.9 = (f32[1,4096]{1,0:T(1,128)S(1)}, f32[1,4096]{1,0:T(1,128)}, u32[]{:S(2)}) copy-start(f32[1,4096]{1,0:T(1,128)} %param.12) | copy-start | bytes 49156
  444.7 193.4 %all-gather.11.cloned.1.call-start = ((), (), s32[]{:S(2)}) async-start(), calls=%async_computation.6 | async-start | bytes 8912896 | tf_op jit(solution)/shard_map/all_gather | solution.py:58
  549.3 2.5 copy-start.5
  549.3 12.6 %collective-permute-start.4 = (bf16[64,4096]{1,0:T(8,128)(2,1)S(1)}, bf16[64,4096]{1,0:T(8,128)(2,1)S(1)}, u32[]{:S(2)}, u32[]{:S(2)}) collective-permute-start(bf16[64,4096]{1,0:T(8,128)(2,1)S(1)} %fusion.9), channel_id=1, source_target_pairs={{0,64},{1,65},{2,66},{3,67},{4,68},{5,69},{6,70},{7,71},{8,72},{9,... | collective-permute-start | bytes 1572872 | tf_op jit(solution)/shard_map/ppermute | solution.py:16
  563.2 0.8 copy-start.3
  565.0 206.0 %reduce-scatter.5.cloned.1.call-start = ((), (), s32[]{:S(2)}) async-start(), calls=%async_computation.7 | async-start | bytes 8912896 | tf_op jit(solution)/shard_map/reduce_scatter | solution.py:66
  638.1 11.1 %copy-start.14 = (bf16[1024,4096]{1,0:T(8,128)(2,1)S(1)}, bf16[1024,4096]{1,0:T(8,128)(2,1)}, u32[]{:S(2)}) copy-start(bf16[1024,4096]{1,0:T(8,128)(2,1)} %all-gather.11.cloned.1.call-done) | copy-start | bytes 25165828
  670.7 0.7 copy-start.15
  671.9 4.7 copy-start.1
  676.6 4.0 copy-start.7
  676.6 4.0 copy-start.8
  680.5 90.5 %copy-start.4 = (bf16[64,4096]{1,0:T(8,128)(2,1)S(1)}, bf16[64,4096]{1,0:T(8,128)(2,1)}, u32[]{:S(2)}) copy-start(bf16[64,4096]{1,0:T(8,128)(2,1)} %copy-done.3) | copy-start | bytes 1572868
  680.5 91.6 %copy-start.6 = (bf16[64,4096]{1,0:T(8,128)(2,1)S(1)}, bf16[64,4096]{1,0:T(8,128)(2,1)}, u32[]{:S(2)}) copy-start(bf16[64,4096]{1,0:T(8,128)(2,1)} %copy-done.5) | copy-start | bytes 1572868
Sparse Core Ops, SparseCore 0:
  11.4 235.5 all-gather.4
  248.6 116.2 all-gather.6
  366.6 66.6 all-gather.8
  444.8 103.1 reduce-scatter.2
  565.1 72.8 all-gather.10
  670.8 100.1 reduce-scatter.4
where the time goes:
time: 781 us; the launch traced here: 780 us
  waiting for transfers between devices  627 us (80%)
  matrix products  62.9 us (8%)
  blocking collectives  35.1 us (4%)
  other arithmetic  24.4 us (3%)
  between operations  14.3 us (2%)
  starting transfers between devices  10.6 us (1%)
    all_gather x2, waiting for transfers between devices, layer(): arrived = lax.all_gather(normed, 'expert', axis=0, tiled=True)  259 us
    reduce_scatter x2, waiting for transfers between devices, layer(): lax.psum_scatter(result, 'expert', scatter_dimension=0, tiled=True)  189 us
    all_gather x1, waiting for transfers between devices, per_device(): full_gate_up = lax.all_gather(gate_up, 'dp', axis=3, tiled=True)  118 us
    all_gather x1, waiting for transfers between devices, per_device(): full_down = lax.all_gather(down_proj, 'dp', axis=2, tiled=True)  49.1 us
    all_gather x1, blocking collectives, per_device(): all_mix = lax.all_gather(dense_mix, 'expert', axis=1, tiled=True)  35.1 us
    dot_general x2, matrix products, layer(): result = jnp.dot(active, down_weights, preferred_element_type=jnp.float32)  23 us
    dot_general x2, matrix products, layer(): up_part = jnp.dot(arrived, up_weights, preferred_element_type=jnp.float32)  22.1 us
    dot_general x2, matrix products, layer(): jnp.dot(arrived, gate_weights, preferred_element_type=jnp.float32)  17.8 us
  transfers between devices with their start and end apart: 11, of which 7 were waited for; matrix products, arithmetic and copies ran while one was open for 6% of the time, Pallas kernels for 0%

commit v1 on v0

--- a/solution.py
+++ b/solution.py
@@ -4,6 +4,32 @@
 from jax.sharding import PartitionSpec as P
 
 EXPERTS = 16
+
+
+def put_islands(buf, row_dim):
+    buf = jnp.moveaxis(buf, 0, row_dim)
+    finding = buf.shape
+    return buf.reshape(
+        *finding[:row_dim], finding[row_dim] * finding[row_dim + 1], *finding[row_dim + 2 :]
+    )
+
+
+def trace_unit(original, row_axis, which_dim):
+    n_slots = lax.axis_size(row_axis)
+    found_now = map(lambda pp: (pp, (pp + 1) % n_slots), range(n_slots))
+    bank = list(found_now)
+    next_value, reply = ([], [])
+    xs_all = [(nth, dd) for dd, nth in bank]
+    for t in [*range(n_slots - 1)]:
+        if t % 2 == 0:
+            passed = lax.ppermute(next_value[-1] if next_value else original, row_axis, bank)
+            next_value.append(passed)
+        else:
+            reply.append(lax.ppermute(reply[-1] if reply else original, row_axis, xs_all))
+    current_value = jnp.stack([*next_value[::-1], original, *reply])
+    latest = lax.axis_index(row_axis) - len(next_value)
+    current_value = current_value[(jnp.arange(n_slots) - latest) % n_slots]
+    return put_islands(current_value, which_dim)
 
 
 def partner(value, axis, bit):
@@ -40,7 +66,7 @@
     own_rank = lax.axis_index("expert")
     section_index = lax.axis_index("section")
     full_gate_up = lax.all_gather(gate_up, "dp", axis=3, tiled=True)
-    full_down = lax.all_gather(down_proj, "dp", axis=2, tiled=True)
+    full_down = trace_unit(down_proj, "dp", 2)
     gate_weights = full_gate_up[0, 0, 0]
     up_weights = full_gate_up[0, 0, 1]
     down_weights = full_down[0, 0]

time: 781 us -> 742 us (0.950)
  waiting for transfers between devices: 627 us -> 561 us
  matrix products: 62.9 us -> 76 us
    all_gather x1 -> x0, waiting for transfers between devices: 49.1 us -> none  [per_device(): full_down = lax.all_gather(down_proj, 'dp', axis=2, tiled=True)]
    all_gather x2, waiting for transfers between devices: 259 us -> 210 us  [layer(): arrived = lax.all_gather(normed, 'expert', axis=0, tiled=True)]
    ppermute x0 -> x3, waiting for transfers between devices: none -> 34.6 us  [the longest x2 34.6 us: trace_unit(): lax.ppermute(next_value[-1] if next_value else original, row_axis, bank)]
    dot_general x2, matrix products: 23 us -> 52 us  [layer(): result = jnp.dot(active, down_weights, preferred_element_type=jnp.float32)]
    dot_general x2 -> x0, matrix products: 17.8 us -> none  [layer(): jnp.dot(arrived, gate_weights, preferred_element_type=jnp.float32)]
  transfers between devices with their start and end apart: 11 -> 13, of which waited for: 7 -> 7; matrix products, arithmetic and copies ran while one was open for 6% -> 9% of each run, Pallas kernels for 0% -> 0%
where the time goes in v1:
time: 742 us; the launch traced here: 741 us
  waiting for transfers between devices  561 us (76%)
  matrix products  76 us (10%)
  blocking collectives  32.8 us (4%)
  other arithmetic  29.7 us (4%)
  starting transfers between devices  15.7 us (2%)
  between operations  14 us (2%)
  local copies, waits for them, and re-layouts  11.9 us (2%)
    all_gather x2, waiting for transfers between devices, layer(): arrived = lax.all_gather(normed, 'expert', axis=0, tiled=True)  210 us
    reduce_scatter x2, waiting for transfers between devices, layer(): lax.psum_scatter(result, 'expert', scatter_dimension=0, tiled=True)  188 us
    all_gather x1, waiting for transfers between devices, per_device(): full_gate_up = lax.all_gather(gate_up, 'dp', axis=3, tiled=True)  117 us
    dot_general x2, matrix products, layer(): result = jnp.dot(active, down_weights, preferred_element_type=jnp.float32)  52 us
    ppermute x2, waiting for transfers between devices, trace_unit(): lax.ppermute(next_value[-1] if next_value else original, row_axis, bank)  34.6 us
    all_gather x1, blocking collectives, per_device(): all_mix = lax.all_gather(dense_mix, 'expert', axis=1, tiled=True)  32.8 us
    dot_general x2, matrix products, layer(): up_part = jnp.dot(arrived, up_weights, preferred_element_type=jnp.float32)  24.1 us
  transfers between devices with their start and end apart: 13, of which 7 were waited for; matrix products, arithmetic and copies ran while one was open for 9% of the time, Pallas kernels for 0%

profile of v1, /device:TPU:0, one launch (start us, length us, event | category | flops | bytes accessed | tf_op | source)
XLA Modules:
  0.0 741.5 jit_solution(15879222643350986988)
XLA Ops:
  7.3 1.5 fusion.6
  9.5 1.7 fusion.8
  12.1 1.7 collective-permute-start
  13.8 1.6 collective-permute-start.2
  15.4 34.6 %collective-permute-done = bf16[1,1,192,4096]{3,2,1,0:T(8,128)(2,1)} collective-permute-done((bf16[1,1,192,4096]{3,2,1,0:T(8,128)(2,1)}, bf16[1,1,192,4096]{3,2,1,0:T(8,128)(2,1)}, u32[]{:S(2)}, u32[]{:S(2)}) %collective-permute-start) | collective-permute-done | bytes 1572896 | tf_op jit(solution)/shard_map/ppermute | solution.py:25
  50.2 3.9 collective-permute-start.4
  54.2 3.5 collective-permute-start.5
  57.8 32.8 %all_gather.14 = f32[2,1024,16]{2,0,1:T(2,128)S(1)} all-gather(f32[2,64,16]{2,0,1:T(2,128)S(1)} %copy.17), channel_id=1, replica_groups=mesh['section'=2,'expert'=16,'dp'=4] {'expert'}, dimensions={1}, use_global_device_ids=true | all-gather | bytes 139264 | tf_op jit(solution)/shard_map/all_gather | solution.py:78
  90.6 1.2 select_reduce_fusion
  91.8 1.1 fusion.19
  92.9 1.2 copy.20
  94.2 1.8 collective-permute-start.6
  96.0 6.6 maximum_bitcast_fusion
  102.5 6.4 gather_fusion
  108.9 137.7 %all-gather.4.cloned.1.call-done = bf16[1024,4096]{1,0:T(8,128)(2,1)} async-done(((bf16[64,4096]{1,0:T(8,128)(2,1)}), bf16[1024,4096]{1,0:T(8,128)(2,1)}) %all-gather.4.cloned.1.call-update) | async-done | bytes 8388624 | tf_op jit(solution)/shard_map/all_gather | solution.py:84
  246.6 117.1 %all-gather.6.cloned.1.call-done = bf16[1,1,2,4096,768]{4,3,2,1,0:T(8,128)(2,1)} async-done(((bf16[1,1,2,1024,768]{4,3,2,1,0:T(8,128)(2,1)}), bf16[1,1,2,4096,768]{4,3,2,1,0:T(8,128)(2,1)}) %all-gather.6.cloned.1.call-update) | async-done | bytes 12582928 | tf_op jit(solution)/shard_map/all_gather | solution.py:68
  363.7 12.0 %fusion.3 = f32[1024,768]{1,0:T(8,128)} fusion(bf16[1024,4096]{1,0:T(8,128)(2,1)} %all-gather.4.cloned.1.call-done, bf16[1,1,2,4096,768]{4,3,2,1,0:T(8,128)(2,1)} %all-gather.6.cloned.1.call-done), kind=kOutput, calls=%fused_computation.9 | convolution fusion | flops 6442450944 | bytes 17825792 | tf_op jit(solution)/shard_map/dot_general | solution.py:86
  375.7 26.0 %multiply_convert_fusion.1 = bf16[1024,4096]{1,0:T(8,128)(2,1)} fusion(f32[1024]{0:T(1024)S(1)} %bitcast.56, bf16[768,4096]{1,0:T(8,128)(2,1)} %bitcast.50, f32[1024,768]{1,0:T(8,128)} %fusion.3, bf16[1024,4096]{1,0:T(8,128)(2,1)} %all-gather.4.cloned.1.call-done, bf16[1,1,2,4096,768]{4,3,2,1,0:T(8,128)(2,1)} %all-gather.6.cloned.1.call-done), kind=kOutput, calls=%fused_computation.2 | convolution fusion | flops 12898009088 | bytes 32509952 | tf_op jit(solution)/shard_map/dot_general | solution.py:88
  401.9 103.5 %reduce-scatter.3.cloned.1.call-done = bf16[64,4096]{1,0:T(8,128)(2,1)} async-done(((bf16[1024,4096]{1,0:T(8,128)(2,1)}), bf16[64,4096]{1,0:T(8,128)(2,1)}) %reduce-scatter.3.cloned.1.call-update) | async-done | bytes 524304 | tf_op jit(solution)/shard_map/reduce_scatter | solution.py:92
  505.4 1.2 fusion.9
  506.6 2.5 collective-permute-start.7
  509.1 10.1 %collective-permute-done.7 = bf16[64,4096]{1,0:T(8,128)(2,1)S(1)} collective-permute-done((bf16[64,4096]{1,0:T(8,128)(2,1)S(1)}, bf16[64,4096]{1,0:T(8,128)(2,1)S(1)}, u32[]{:S(2)}, u32[]{:S(2)}) %collective-permute-start.7) | collective-permute-done | bytes 524320 | tf_op jit(solution)/shard_map/ppermute | solution.py:42
  520.3 1.0 fusion.12
  521.8 72.6 %all-gather.8.cloned.1.call-done = bf16[1024,4096]{1,0:T(8,128)(2,1)} async-done(((bf16[64,4096]{1,0:T(8,128)(2,1)}), bf16[1024,4096]{1,0:T(8,128)(2,1)}) %all-gather.8.cloned.1.call-update) | async-done | bytes 8388624 | tf_op jit(solution)/shard_map/all_gather | solution.py:84
  594.3 12.0 %fusion.2 = f32[1024,768]{1,0:T(8,128)} fusion(bf16[1024,4096]{1,0:T(8,128)(2,1)} %all-gather.8.cloned.1.call-done, bf16[1,1,2,4096,768]{4,3,2,1,0:T(8,128)(2,1)} %all-gather.6.cloned.1.call-done), kind=kOutput, calls=%fused_computation.8 | convolution fusion | flops 6442450944 | bytes 17825792 | tf_op jit(solution)/shard_map/dot_general | solution.py:86
  606.4 26.0 %multiply_convert_fusion = bf16[1024,4096]{1,0:T(8,128)(2,1)} fusion(f32[1024]{0:T(1024)S(1)} %bitcast.57, bf16[768,4096]{1,0:T(8,128)(2,1)} %bitcast.51, f32[1024,768]{1,0:T(8,128)} %fusion.2, bf16[1024,4096]{1,0:T(8,128)(2,1)} %all-gather.8.cloned.1.call-done, bf16[1,1,2,4096,768]{4,3,2,1,0:T(8,128)(2,1)} %all-gather.6.cloned.1.call-done), kind=kOutput, calls=%fused_computation.1 | convolution fusion | flops 12898009088 | bytes 32509952 | tf_op jit(solution)/shard_map/dot_general | solution.py:88
  634.2 4.8 broadcast_select_fusion
  639.1 3.7 broadcast_select_fusion.3
  642.8 5.0 broadcast_select_fusion.1
  647.7 84.9 %reduce-scatter.5.cloned.1.call-done = bf16[64,4096]{1,0:T(8,128)(2,1)} async-done(((bf16[1024,4096]{1,0:T(8,128)(2,1)}), bf16[64,4096]{1,0:T(8,128)(2,1)}) %reduce-scatter.5.cloned.1.call-update) | async-done | bytes 524304 | tf_op jit(solution)/shard_map/reduce_scatter | solution.py:92
  732.7 1.2 fusion.14
  733.9 1.1 maximum_bitcast_fusion.1
  (64 shorter events, 5.7 us)
Async XLA Ops:
  7.2 47.0 %copy-start = (bf16[1,1,2,1024,768]{4,3,2,1,0:T(8,128)(2,1)S(1)}, bf16[1,1,2,1024,768]{4,3,2,1,0:T(8,128)(2,1)}, u32[]{:S(2)}) copy-start(bf16[1,1,2,1024,768]{4,3,2,1,0:T(8,128)(2,1)} %param.13) | copy-start | bytes 9437188
  7.2 50.5 %copy-start.14 = (f32[1,2,64,8]{2,3,1,0:T(8,128)S(1)}, f32[1,2,64,8]{2,3,1,0:T(8,128)}, u32[]{:S(2)}) copy-start(f32[1,2,64,8]{2,3,1,0:T(8,128)} %param.18) | copy-start | bytes 12292
  7.2 50.5 %copy-start.15 = (s32[1,2,64,8]{2,3,1,0:T(8,128)S(1)}, s32[1,2,64,8]{2,3,1,0:T(8,128)}, u32[]{:S(2)}) copy-start(s32[1,2,64,8]{2,3,1,0:T(8,128)} %param.17) | copy-start | bytes 12292
  7.2 239.4 %all-gather.4.cloned.1.call-start = ((), (), s32[]{:S(2)}) async-start(), calls=%async_computation.2 | async-start | bytes 8912896 | tf_op jit(solution)/shard_map/all_gather | solution.py:84
  8.7 0.8 copy-start.3
  11.3 352.4 %all-gather.6.cloned.1.call-start = ((), (), s32[]{:S(2)}) async-start(), calls=%async_computation.3 | async-start | bytes 15728640 | tf_op jit(solution)/shard_map/all_gather | solution.py:68
  12.0 493.4 %reduce-scatter.3.cloned.1.call-start = ((), (), s32[]{:S(2)}) async-start(), calls=%async_computation.4 | async-start | bytes 8912896 | tf_op jit(solution)/shard_map/reduce_scatter | solution.py:92
  12.1 37.9 %collective-permute-start = (bf16[1,1,192,4096]{3,2,1,0:T(8,128)(2,1)}, bf16[1,1,192,4096]{3,2,1,0:T(8,128)(2,1)}, u32[]{:S(2)}, u32[]{:S(2)}) collective-permute-start(bf16[1,1,192,4096]{3,2,1,0:T(8,128)(2,1)} %param.14), channel_id=1, source_target_pairs={{0,1},{1,2},{2,3},{3,0},{4,5},{5,6},{6,7},{7,4},{8,9},{9,10},{10,1... | collective-permute-start | bytes 4718600 | tf_op jit(solution)/shard_map/ppermute | solution.py:25
  13.8 80.4 %collective-permute-start.2 = (bf16[1,1,192,4096]{3,2,1,0:T(8,128)(2,1)}, bf16[1,1,192,4096]{3,2,1,0:T(8,128)(2,1)}, u32[]{:S(2)}, u32[]{:S(2)}) collective-permute-start(bf16[1,1,192,4096]{3,2,1,0:T(8,128)(2,1)} %param.14), channel_id=1, source_target_pairs={{1,0},{2,1},{3,2},{0,3},{5,4},{6,5},{7,6},{4,7},{9,8},{10,9},{11,1... | collective-permute-start | bytes 4718600 | tf_op jit(solution)/shard_map/ppermute | solution.py:28
  49.9 46.0 %collective-permute-start.1 = (bf16[1,1,192,4096]{3,2,1,0:T(8,128)(2,1)}, bf16[1,1,192,4096]{3,2,1,0:T(8,128)(2,1)}, u32[]{:S(2)}, u32[]{:S(2)}) collective-permute-start(bf16[1,1,192,4096]{3,2,1,0:T(8,128)(2,1)} %collective-permute-done), channel_id=1, source_target_pairs={{0,1},{1,2},{2,3},{3,0},{4,5},{5,6},{6,7},{7,4},{8,9},{9,10},{10,1... | collective-permute-start | bytes 4718600 | tf_op jit(solution)/shard_map/ppermute | solution.py:25
  50.2 351.5 %collective-permute-start.4 = (bf16[1,1,192,4096]{3,2,1,0:T(8,128)(2,1)}, bf16[1,1,192,4096]{3,2,1,0:T(8,128)(2,1)}, u32[]{:S(2)}, u32[]{:S(2)}) collective-permute-start(bf16[1,1,192,4096]{3,2,1,0:T(8,128)(2,1)} %param.14), channel_id=1, source_target_pairs={{0,32},{4,36},{8,40},{12,44},{16,48},{20,52},{24,56},{28,60},{32,0... | collective-permute-start | bytes 4718600 | tf_op jit(solution)/shard_map/ppermute | solution.py:36
  54.1 347.6 %collective-permute-start.3 = (bf16[1,1,2,1024,768]{4,3,2,1,0:T(8,128)(2,1)S(1)}, bf16[1,1,2,1024,768]{4,3,2,1,0:T(8,128)(2,1)}, u32[]{:S(2)}, u32[]{:S(2)}) collective-permute-start(bf16[1,1,2,1024,768]{4,3,2,1,0:T(8,128)(2,1)S(1)} %copy-done), channel_id=1, source_target_pairs={{0,32},{4,36},{8,40},{12,44},{16,48},{20,52},{24,56},{28,60},{32,0... | collective-permute-start | bytes 9437192 | tf_op jit(solution)/shard_map/ppermute | solution.py:36
  54.2 347.6 %collective-permute-start.5 = (bf16[1,1,192,4096]{3,2,1,0:T(8,128)(2,1)}, bf16[1,1,192,4096]{3,2,1,0:T(8,128)(2,1)}, u32[]{:S(2)}, u32[]{:S(2)}) collective-permute-start(bf16[1,1,192,4096]{3,2,1,0:T(8,128)(2,1)} %param.15), channel_id=1, source_target_pairs={{0,32},{4,36},{8,40},{12,44},{16,48},{20,52},{24,56},{28,60},{32,0... | collective-permute-start | bytes 4718600 | tf_op jit(solution)/shard_map/ppermute | solution.py:36
  94.2 307.6 %collective-permute-start.6 = (bf16[1,1,192,4096]{3,2,1,0:T(8,128)(2,1)}, bf16[1,1,192,4096]{3,2,1,0:T(8,128)(2,1)}, u32[]{:S(2)}, u32[]{:S(2)}) collective-permute-start(bf16[1,1,192,4096]{3,2,1,0:T(8,128)(2,1)} %param.16), channel_id=1, source_target_pairs={{0,32},{4,36},{8,40},{12,44},{16,48},{20,52},{24,56},{28,60},{32,0... | collective-permute-start | bytes 4718600 | tf_op jit(solution)/shard_map/ppermute | solution.py:36
  401.7 118.6 %copy-start.13 = (f32[1,4096]{1,0:T(1,128)S(1)}, f32[1,4096]{1,0:T(1,128)}, u32[]{:S(2)}) copy-start(f32[1,4096]{1,0:T(1,128)} %param.12) | copy-start | bytes 49156
  401.8 103.6 %copy-start.4 = (bf16[64,4096]{1,0:T(8,128)(2,1)S(1)}, bf16[64,4096]{1,0:T(8,128)(2,1)}, u32[]{:S(2)}) copy-start(bf16[64,4096]{1,0:T(8,128)(2,1)} %copy-done.3) | copy-start | bytes 1572868
  401.8 117.4 %copy-start.12 = (bf16[2,64,4096]{2,1,0:T(8,128)(2,1)S(1)}, bf16[2,64,4096]{2,1,0:T(8,128)(2,1)}, u32[]{:S(2)}) copy-start(bf16[2,64,4096]{2,1,0:T(8,128)(2,1)} %param.10) | copy-start | bytes 3145732
  401.8 119.8 %copy-start.9 = (f32[1,1024]{0,1:T(8,128)S(1)}, f32[1,1024]{0,1:T(8,128)}, u32[]{:S(2)}) copy-start(f32[1,1024]{0,1:T(8,128)} %get-tuple-element.20) | copy-start | bytes 12292
  401.8 192.5 %all-gather.8.cloned.1.call-start = ((), (), s32[]{:S(2)}) async-start(), calls=%async_computation.5 | async-start | bytes 8912896 | tf_op jit(solution)/shard_map/all_gather | solution.py:84
  506.6 2.5 copy-start.7
  506.6 12.6 %collective-permute-start.7 = (bf16[64,4096]{1,0:T(8,128)(2,1)S(1)}, bf16[64,4096]{1,0:T(8,128)(2,1)S(1)}, u32[]{:S(2)}, u32[]{:S(2)}) collective-permute-start(bf16[64,4096]{1,0:T(8,128)(2,1)S(1)} %fusion.9), channel_id=1, source_target_pairs={{0,64},{1,65},{2,66},{3,67},{4,68},{5,69},{6,70},{7,71},{8,72},{9,... | collective-permute-start | bytes 1572872 | tf_op jit(solution)/shard_map/ppermute | solution.py:42
  519.5 0.8 copy-start.5
  521.3 211.4 %reduce-scatter.5.cloned.1.call-start = ((), (), s32[]{:S(2)}) async-start(), calls=%async_computation.6 | async-start | bytes 8912896 | tf_op jit(solution)/shard_map/reduce_scatter | solution.py:92
  632.3 0.7 copy-start.16
  632.3 1.9 copy-start.1
  633.0 6.1 copy-start.2
  634.2 8.5 %copy-start.10 = (bf16[1,1,192,4096]{3,2,1,0:T(8,128)(2,1)S(1)}, bf16[1,1,192,4096]{3,2,1,0:T(8,128)(2,1)}, u32[]{:S(2)}) copy-start(bf16[1,1,192,4096]{3,2,1,0:T(8,128)(2,1)} %param.16) | copy-start | bytes 4718596
  634.2 8.5 %copy-start.11 = (bf16[1,1,192,4096]{3,2,1,0:T(8,128)(2,1)S(1)}, bf16[1,1,192,4096]{3,2,1,0:T(8,128)(2,1)}, u32[]{:S(2)}) copy-start(bf16[1,1,192,4096]{3,2,1,0:T(8,128)(2,1)} %param.15) | copy-start | bytes 4718596
  639.1 93.6 %copy-start.6 = (bf16[64,4096]{1,0:T(8,128)(2,1)S(1)}, bf16[64,4096]{1,0:T(8,128)(2,1)}, u32[]{:S(2)}) copy-start(bf16[64,4096]{1,0:T(8,128)(2,1)} %copy-done.5) | copy-start | bytes 1572868
  642.8 91.1 %copy-start.8 = (bf16[64,4096]{1,0:T(8,128)(2,1)S(1)}, bf16[64,4096]{1,0:T(8,128)(2,1)}, u32[]{:S(2)}) copy-start(bf16[64,4096]{1,0:T(8,128)(2,1)} %copy-done.7) | copy-start | bytes 1572868
Sparse Core Ops, SparseCore 0:
  11.4 235.1 all-gather.3
  248.3 115.3 all-gather.5
  401.9 103.4 reduce-scatter.2
  521.4 72.8 all-gather.7
  632.5 100.1 reduce-scatter.4
